TPU v7x, 32 devices: a whole 2x2x4 slice. The times are simulated.
32 devices in a mesh: dp: 4 (over y, x), fsdp: 8 (over z, core).
Axes of the slice: x: 2, y: 2, z: 4, core: 2. Of those that a mesh axis runs over, the one named last changes fastest.
Arguments:
- stream_x: bfloat16 [32768, 512], P(('dp', 'fsdp')), may hold values from -6 to 6
- stream_y: bfloat16 [32768, 512], P(('dp', 'fsdp')), may hold values from -6 to 6
- cotangent: bfloat16 [32768, 512], P(('dp', 'fsdp')), may hold values from -6 to 6
- doc_lengths: int32 [32, 16], P(('dp', 'fsdp')), may hold values from 1 to 512, 1024 in all within a row
- query_weight: bfloat16 [512, 512], P(('dp', 'fsdp')), may hold values from -0.25 to 0.25
- query_bias: bfloat16 [512], P(('dp', 'fsdp')), may hold values from -2.5 to 2.5
- key_weight: bfloat16 [512, 512], P(('dp', 'fsdp')), may hold values from -0.25 to 0.25
- value_weight: bfloat16 [512, 512], P(('dp', 'fsdp')), may hold values from -0.25 to 0.25
- value_bias: bfloat16 [512], P(('dp', 'fsdp')), may hold values from -3 to 3
- output_weight: bfloat16 [512, 512], P(('dp', 'fsdp')), may hold values from -1 to 1
- output_bias: bfloat16 [512], P(('dp', 'fsdp')), may hold values from -2.5 to 2.5
- first_gain: bfloat16 [512], P(('dp', 'fsdp')), may hold values from 0.099609375 to 1.8984375
- first_shift: bfloat16 [512], P(('dp', 'fsdp')), may hold values from -2.5 to 2.5
- up_weight: bfloat16 [512, 2048], P(('dp', 'fsdp')), may hold values from -0.25 to 0.25
- up_bias: bfloat16 [2048], P(('dp', 'fsdp')), may hold values from -3 to 3
- down_weight: bfloat16 [2048, 512], P(('dp', 'fsdp')), may hold values from -0.1875 to 0.1875
- down_bias: bfloat16 [512], P(('dp', 'fsdp')), may hold values from -2.5 to 2.5
- second_gain: bfloat16 [512], P(('dp', 'fsdp')), may hold values from 0.099609375 to 1.8984375
- second_shift: bfloat16 [512], P(('dp', 'fsdp')), may hold values from -2.5 to 2.5
- final_gain: bfloat16 [512], P(('dp', 'fsdp')), may hold values from 0.099609375 to 1.8984375
- final_shift: bfloat16 [512], P(('dp', 'fsdp')), may hold values from -2.5 to 2.5
Outputs:
- block_out: bfloat16 [32768, 512], P(('dp', 'fsdp'))
- grad_x: float32 [32768, 512], P(('dp', 'fsdp'))
- grad_y: float32 [32768, 512], P(('dp', 'fsdp'))
- query_weight_grad: float32 [512, 512], P(('dp', 'fsdp'))
- query_bias_grad: float32 [512], P(('dp', 'fsdp'))
- key_weight_grad: float32 [512, 512], P(('dp', 'fsdp'))
- value_weight_grad: float32 [512, 512], P(('dp', 'fsdp'))
- value_bias_grad: float32 [512], P(('dp', 'fsdp'))
- output_weight_grad: float32 [512, 512], P(('dp', 'fsdp'))
- output_bias_grad: float32 [512], P(('dp', 'fsdp'))
- first_gain_grad: float32 [512], P(('dp', 'fsdp'))
- first_shift_grad: float32 [512], P(('dp', 'fsdp'))
- up_weight_grad: float32 [512, 2048], P(('dp', 'fsdp'))
- up_bias_grad: float32 [2048], P(('dp', 'fsdp'))
- down_weight_grad: float32 [2048, 512], P(('dp', 'fsdp'))
- down_bias_grad: float32 [512], P(('dp', 'fsdp'))
- second_gain_grad: float32 [512], P(('dp', 'fsdp'))
- second_shift_grad: float32 [512], P(('dp', 'fsdp'))
- final_gain_grad: float32 [512], P(('dp', 'fsdp'))
- final_shift_grad: float32 [512], P(('dp', 'fsdp'))
Inputs may be any that keep to these rules, and one draw needn't show every extreme that they name: `doc_lengths`: row p lists the lengths of the 16 sequences packed in order into the 1024 tokens of pack p; each row sums to 1024, and the longest of every row is exactly 512.
All inputs are finite; a program needn't handle non-finite values.
Results may differ from a plain program's by a relative error of at most 0.012.
The roundings to bfloat16 on the way count: a program that leaves them out, or rounds other values in their place, can miss the bound.
Values may be sent and summed in bfloat16 or wider, within the bound.
No kernel may reach another device: no remote copies, remote signals or barrier semaphores. Data moves between devices by JAX's collectives and lax.ppermute only.
A program may use at most 128 MiB of HBM per device.

v0:
```python
import math

import jax
import jax.numpy as jnp
from jax import lax
from jax.sharding import PartitionSpec as P

HEADS = 8


epsilon = 1e-05
neg_large = -1e30


def normalize(values):
    centre = jnp.mean(values, axis=-1, keepdims=True)
    shifted = values - centre
    spread = jnp.mean(shifted * shifted, axis=-1, keepdims=True)
    scaler = lax.rsqrt(spread + epsilon)
    return (shifted * scaler, scaler)


def norm_back(upstream, normed, scaler):
    return scaler * (
        upstream
        - jnp.mean(upstream, axis=-1, keepdims=True)
        - normed * jnp.mean(upstream * normed, axis=-1, keepdims=True)
    )


def gelu_exact(values):
    return 0.5 * values * (1.0 + lax.erf(values * 0.7071067811865476))


def gelu_slope(values):
    return (
        0.5 * (1.0 + lax.erf(values * 0.7071067811865476))
        + values * jnp.exp(-0.5 * values * values) * 0.3989422804014327
    )


def project(inputs, weight):
    return jnp.dot(inputs, weight, preferred_element_type=jnp.float32)


def project_back(gradients, weight):
    return jnp.einsum("te,de->td", gradients, weight, preferred_element_type=jnp.float32)


def outer_sum(inputs, gradients):
    return jnp.einsum("td,te->de", inputs, gradients, preferred_element_type=jnp.float32)


def column_sum(gradients):
    return jnp.sum(gradients.astype(jnp.float32), axis=0)


def block_scores(queries, keys, position, segment, offset, block_rows, factor):
    chosen = lax.dynamic_slice_in_dim(queries, offset, block_rows, 0)
    row_position = lax.dynamic_slice_in_dim(position, offset, block_rows, 0)
    row_segment = lax.dynamic_slice_in_dim(segment, offset, block_rows, 0)
    visible = (row_segment[:, None] == segment[None, :]) & (
        row_position[:, None] >= position[None, :]
    )
    scores = jnp.einsum("bhd,khd->hbk", chosen, keys, preferred_element_type=jnp.float32) * factor
    return (jnp.where(visible[None], scores, neg_large), chosen)


def body(
    stream_x,
    stream_y,
    cotangent,
    doc_lengths,
    query_weight,
    query_bias,
    key_weight,
    value_weight,
    value_bias,
    output_weight,
    output_bias,
    first_gain,
    first_shift,
    up_weight,
    up_bias,
    down_weight,
    down_bias,
    second_gain,
    second_shift,
    final_gain,
    final_shift,
):
    length, width = stream_x.shape
    heads = HEADS
    head_size = width // heads
    factor = 1.0 / math.sqrt(head_size)
    block_rows = min(512, length)
    blocks = length // block_rows
    bounds = jnp.cumsum(doc_lengths[0])
    position = jnp.arange(length, dtype=jnp.int32)
    segment = jnp.sum((position[:, None] >= bounds[None, :]).astype(jnp.int32), axis=1)
    (
        whole_query,
        whole_key,
        whole_value,
        whole_output,
        bias_query,
        bias_value,
        bias_output,
        gain_first,
        shift_first,
    ) = (
        lax.all_gather(query_weight, ("dp", "fsdp"), axis=0, tiled=True),
        lax.all_gather(key_weight, ("dp", "fsdp"), axis=0, tiled=True),
        lax.all_gather(value_weight, ("dp", "fsdp"), axis=0, tiled=True),
        lax.all_gather(output_weight, ("dp", "fsdp"), axis=0, tiled=True),
        lax.all_gather(query_bias, ("dp", "fsdp"), axis=0, tiled=True),
        lax.all_gather(value_bias, ("dp", "fsdp"), axis=0, tiled=True),
        lax.all_gather(output_bias, ("dp", "fsdp"), axis=0, tiled=True),
        lax.all_gather(first_gain, ("dp", "fsdp"), axis=0, tiled=True),
        lax.all_gather(first_shift, ("dp", "fsdp"), axis=0, tiled=True),
    )
    queries = (
        (project(stream_x, whole_query) + bias_query)
        .astype(jnp.bfloat16)
        .reshape(length, heads, head_size)
    )
    keys = project(stream_x, whole_key).astype(jnp.bfloat16).reshape(length, heads, head_size)
    values = (
        (project(stream_x, whole_value) + bias_value)
        .astype(jnp.bfloat16)
        .reshape(length, heads, head_size)
    )

    def attend(number):
        offset = number * block_rows
        scores, chosen = block_scores(queries, keys, position, segment, offset, block_rows, factor)
        peaks = jnp.max(scores, axis=-1, keepdims=True)
        expon = jnp.exp(scores - peaks)
        totals = jnp.sum(expon, axis=-1, keepdims=True)
        weights = (expon / totals).astype(jnp.bfloat16)
        mixed = jnp.einsum("hbk,khd->bhd", weights, values, preferred_element_type=jnp.float32)
        return (mixed, (peaks + jnp.log(totals))[:, :, 0])

    contexts, logsums = lax.map(attend, jnp.arange(blocks))
    context = contexts.reshape(length, width).astype(jnp.bfloat16)
    branch = project(context, whole_output) + bias_output
    first_normed, first_scale = normalize(stream_x.astype(jnp.float32) + branch)
    first_out = first_normed * gain_first + shift_first
    mid_y = stream_y.astype(jnp.float32) + branch
    whole_up, whole_down, bias_up, bias_down, gain_second, shift_second, gain_final, shift_final = (
        lax.all_gather(up_weight, ("dp", "fsdp"), axis=0, tiled=True),
        lax.all_gather(down_weight, ("dp", "fsdp"), axis=0, tiled=True),
        lax.all_gather(up_bias, ("dp", "fsdp"), axis=0, tiled=True),
        lax.all_gather(down_bias, ("dp", "fsdp"), axis=0, tiled=True),
        lax.all_gather(second_gain, ("dp", "fsdp"), axis=0, tiled=True),
        lax.all_gather(second_shift, ("dp", "fsdp"), axis=0, tiled=True),
        lax.all_gather(final_gain, ("dp", "fsdp"), axis=0, tiled=True),
        lax.all_gather(final_shift, ("dp", "fsdp"), axis=0, tiled=True),
    )
    first_low = first_out.astype(jnp.bfloat16)
    hidden_pre = project(first_low, whole_up) + bias_up
    hidden = gelu_exact(hidden_pre).astype(jnp.bfloat16)
    feed = project(hidden, whole_down) + bias_down
    second_normed, second_scale = normalize(first_out + feed)
    final_y = mid_y + feed
    final_normed, final_scale = normalize(final_y)
    block_out = (
        second_normed * gain_second + shift_second + final_normed * gain_final + shift_final
    ).astype(jnp.bfloat16)
    whole_up, whole_down, bias_up, bias_down, gain_second, shift_second, gain_final, shift_final = (
        lax.all_gather(up_weight, ("dp", "fsdp"), axis=0, tiled=True),
        lax.all_gather(down_weight, ("dp", "fsdp"), axis=0, tiled=True),
        lax.all_gather(up_bias, ("dp", "fsdp"), axis=0, tiled=True),
        lax.all_gather(down_bias, ("dp", "fsdp"), axis=0, tiled=True),
        lax.all_gather(second_gain, ("dp", "fsdp"), axis=0, tiled=True),
        lax.all_gather(second_shift, ("dp", "fsdp"), axis=0, tiled=True),
        lax.all_gather(final_gain, ("dp", "fsdp"), axis=0, tiled=True),
        lax.all_gather(final_shift, ("dp", "fsdp"), axis=0, tiled=True),
    )
    upstream = cotangent.astype(jnp.float32)
    final_gain_grad = jnp.sum(upstream * final_normed, axis=0)
    final_shift_grad = jnp.sum(upstream, axis=0)
    second_gain_grad = jnp.sum(upstream * second_normed, axis=0)
    stream_y_grad = norm_back(upstream * gain_final, final_normed, final_scale)
    second_back = norm_back(upstream * gain_second, second_normed, second_scale)
    feed_grad = (second_back + stream_y_grad).astype(jnp.bfloat16)
    down_bias_grad = column_sum(feed_grad)
    down_weight_grad = outer_sum(hidden, feed_grad)
    hidden_grad = (project_back(feed_grad, whole_down) * gelu_slope(hidden_pre)).astype(
        jnp.bfloat16
    )
    up_bias_grad = column_sum(hidden_grad)
    up_weight_grad = outer_sum(first_low, hidden_grad)
    first_grad = second_back + project_back(hidden_grad, whole_up)
    (
        whole_query,
        whole_key,
        whole_value,
        whole_output,
        bias_query,
        bias_value,
        bias_output,
        gain_first,
        shift_first,
    ) = (
        lax.all_gather(query_weight, ("dp", "fsdp"), axis=0, tiled=True),
        lax.all_gather(key_weight, ("dp", "fsdp"), axis=0, tiled=True),
        lax.all_gather(value_weight, ("dp", "fsdp"), axis=0, tiled=True),
        lax.all_gather(output_weight, ("dp", "fsdp"), axis=0, tiled=True),
        lax.all_gather(query_bias, ("dp", "fsdp"), axis=0, tiled=True),
        lax.all_gather(value_bias, ("dp", "fsdp"), axis=0, tiled=True),
        lax.all_gather(output_bias, ("dp", "fsdp"), axis=0, tiled=True),
        lax.all_gather(first_gain, ("dp", "fsdp"), axis=0, tiled=True),
        lax.all_gather(first_shift, ("dp", "fsdp"), axis=0, tiled=True),
    )
    first_gain_grad = jnp.sum(first_grad * first_normed, axis=0)
    first_shift_grad = jnp.sum(first_grad, axis=0)
    first_back = norm_back(first_grad * gain_first, first_normed, first_scale)
    branch_grad = (first_back + stream_y_grad).astype(jnp.bfloat16)
    output_bias_grad = column_sum(branch_grad)
    output_weight_grad = outer_sum(context, branch_grad)
    context_grad = (
        project_back(branch_grad, whole_output)
        .astype(jnp.bfloat16)
        .reshape(length, heads, head_size)
    )

    def attend_back(carry, number):
        key_total, value_total = carry
        offset = number * block_rows
        scores, chosen = block_scores(queries, keys, position, segment, offset, block_rows, factor)
        logsum = lax.dynamic_index_in_dim(logsums, number, 0, keepdims=False)
        attention = jnp.exp(scores - logsum[:, :, None])
        incoming = lax.dynamic_slice_in_dim(context_grad, offset, block_rows, 0)
        weight_grad = jnp.einsum(
            "bhd,khd->hbk", incoming, values, preferred_element_type=jnp.float32
        )
        balance = jnp.sum(attention * weight_grad, axis=-1, keepdims=True)
        score_grad = (attention * (weight_grad - balance)).astype(jnp.bfloat16)
        query_part = (
            jnp.einsum("hbk,khd->bhd", score_grad, keys, preferred_element_type=jnp.float32)
            * factor
        )
        key_total = (
            key_total
            + jnp.einsum("hbk,bhd->khd", score_grad, chosen, preferred_element_type=jnp.float32)
            * factor
        )
        value_total = value_total + jnp.einsum(
            "hbk,bhd->khd",
            attention.astype(jnp.bfloat16),
            incoming,
            preferred_element_type=jnp.float32,
        )
        return ((key_total, value_total), query_part)

    zeros = jnp.zeros((length, heads, head_size), jnp.float32)
    (key_total, value_total), query_parts = lax.scan(
        attend_back, (zeros, zeros), jnp.arange(blocks)
    )
    query_grad = query_parts.reshape(length, width).astype(jnp.bfloat16)
    key_grad = key_total.reshape(length, width).astype(jnp.bfloat16)
    value_grad = value_total.reshape(length, width).astype(jnp.bfloat16)
    query_bias_grad = column_sum(query_grad)
    value_bias_grad = column_sum(value_grad)
    query_weight_grad = outer_sum(stream_x, query_grad)
    key_weight_grad = outer_sum(stream_x, key_grad)
    value_weight_grad = outer_sum(stream_x, value_grad)
    input_grad = (
        first_back
        + project_back(query_grad, whole_query)
        + project_back(key_grad, whole_key)
        + project_back(value_grad, whole_value)
    )
    (
        query_weight_share,
        key_weight_share,
        value_weight_share,
        output_weight_share,
        query_bias_share,
        value_bias_share,
        output_bias_share,
        first_gain_share,
        first_shift_share,
        up_weight_share,
        down_weight_share,
        up_bias_share,
        down_bias_share,
        second_gain_share,
        second_shift_share,
        final_gain_share,
        final_shift_share,
    ) = (
        lax.psum_scatter(query_weight_grad, ("dp", "fsdp"), scatter_dimension=0, tiled=True),
        lax.psum_scatter(key_weight_grad, ("dp", "fsdp"), scatter_dimension=0, tiled=True),
        lax.psum_scatter(value_weight_grad, ("dp", "fsdp"), scatter_dimension=0, tiled=True),
        lax.psum_scatter(output_weight_grad, ("dp", "fsdp"), scatter_dimension=0, tiled=True),
        lax.psum_scatter(query_bias_grad, ("dp", "fsdp"), scatter_dimension=0, tiled=True),
        lax.psum_scatter(value_bias_grad, ("dp", "fsdp"), scatter_dimension=0, tiled=True),
        lax.psum_scatter(output_bias_grad, ("dp", "fsdp"), scatter_dimension=0, tiled=True),
        lax.psum_scatter(first_gain_grad, ("dp", "fsdp"), scatter_dimension=0, tiled=True),
        lax.psum_scatter(first_shift_grad, ("dp", "fsdp"), scatter_dimension=0, tiled=True),
        lax.psum_scatter(up_weight_grad, ("dp", "fsdp"), scatter_dimension=0, tiled=True),
        lax.psum_scatter(down_weight_grad, ("dp", "fsdp"), scatter_dimension=0, tiled=True),
        lax.psum_scatter(up_bias_grad, ("dp", "fsdp"), scatter_dimension=0, tiled=True),
        lax.psum_scatter(down_bias_grad, ("dp", "fsdp"), scatter_dimension=0, tiled=True),
        lax.psum_scatter(second_gain_grad, ("dp", "fsdp"), scatter_dimension=0, tiled=True),
        lax.psum_scatter(final_shift_grad, ("dp", "fsdp"), scatter_dimension=0, tiled=True),
        lax.psum_scatter(final_gain_grad, ("dp", "fsdp"), scatter_dimension=0, tiled=True),
        lax.psum_scatter(final_shift_grad, ("dp", "fsdp"), scatter_dimension=0, tiled=True),
    )
    return (
        block_out,
        input_grad,
        stream_y_grad,
        query_weight_share,
        query_bias_share,
        key_weight_share,
        value_weight_share,
        value_bias_share,
        output_weight_share,
        output_bias_share,
        first_gain_share,
        first_shift_share,
        up_weight_share,
        up_bias_share,
        down_weight_share,
        down_bias_share,
        second_gain_share,
        second_shift_share,
        final_gain_share,
        final_shift_share,
    )


def solution(mesh):
    placed = (
        P(("dp", "fsdp"), None),
        P(("dp", "fsdp"), None),
        P(("dp", "fsdp"), None),
        P(("dp", "fsdp"), None),
        P(("dp", "fsdp"), None),
        P(("dp", "fsdp")),
        P(("dp", "fsdp"), None),
        P(("dp", "fsdp"), None),
        P(("dp", "fsdp")),
        P(("dp", "fsdp"), None),
        P(("dp", "fsdp")),
        P(("dp", "fsdp")),
        P(("dp", "fsdp")),
        P(("dp", "fsdp"), None),
        P(("dp", "fsdp")),
        P(("dp", "fsdp"), None),
        P(("dp", "fsdp")),
        P(("dp", "fsdp")),
        P(("dp", "fsdp")),
        P(("dp", "fsdp")),
        P(("dp", "fsdp")),
    )
    return jax.shard_map(
        body,
        mesh=mesh,
        in_specs=placed,
        out_specs=(
            P(("dp", "fsdp"), None),
            P(("dp", "fsdp"), None),
            P(("dp", "fsdp"), None),
            P(("dp", "fsdp"), None),
            P(("dp", "fsdp")),
            P(("dp", "fsdp"), None),
            P(("dp", "fsdp"), None),
            P(("dp", "fsdp")),
            P(("dp", "fsdp"), None),
            P(("dp", "fsdp")),
            P(("dp", "fsdp")),
            P(("dp", "fsdp")),
            P(("dp", "fsdp"), None),
            P(("dp", "fsdp")),
            P(("dp", "fsdp"), None),
            P(("dp", "fsdp")),
            P(("dp", "fsdp")),
            P(("dp", "fsdp")),
            P(("dp", "fsdp")),
            P(("dp", "fsdp")),
        ),
        check_vma=False,
    )
```

profile of v0, /device:TPU:0, one launch (start us, length us, event | category | flops | bytes accessed | tf_op | source)
XLA Modules:
  0.0 1138.6 jit_solution(17601982182794395152)
XLA Ops:
  18.1 42.4 %all-reduce.22 = (bf16[512]{0:T(512)(128)(2,1)S(1)}, bf16[512]{0:T(512)(128)(2,1)S(1)}, bf16[512]{0:T(512)(128)(2,1)}, bf16[512]{0:T(512)(128)(2,1)}, bf16[512]{...) all-reduce(bf16[512]{0:T(512)(128)(2,1)S(1)} %dynamic-update-slice,, ...), channel_id=1, replica_groups=mesh['dp'=4,'fsdp'=8] {'dp','fsdp'}, use_global_device_ids=true, to_apply=%add | all-reduce | flops 7168 | bytes 28672
  61.4 43.6 %all_gather.60 = bf16[512,512]{1,0:T(8,128)(2,1)S(1)} all-gather(bf16[16,512]{1,0:T(8,128)(2,1)} %param.29), channel_id=1, replica_groups=mesh['dp'=4,'fsdp'=8] {'dp','fsdp'}, dimensions={0}, use_global_device_ids=true | all-gather | bytes 540672 | tf_op jit(solution)/shard_map/all_gather | solution.py:112
  105.1 39.5 %all_gather.62 = bf16[512,512]{1,0:T(8,128)(2,1)S(1)} all-gather(bf16[16,512]{1,0:T(8,128)(2,1)} %param.31), channel_id=1, replica_groups=mesh['dp'=4,'fsdp'=8] {'dp','fsdp'}, dimensions={0}, use_global_device_ids=true | all-gather | bytes 540672 | tf_op jit(solution)/shard_map/all_gather | solution.py:113
  144.6 40.8 %all_gather.63 = bf16[512,512]{1,0:T(8,128)(2,1)S(1)} all-gather(bf16[16,512]{1,0:T(8,128)(2,1)} %param.32), channel_id=1, replica_groups=mesh['dp'=4,'fsdp'=8] {'dp','fsdp'}, dimensions={0}, use_global_device_ids=true | all-gather | bytes 540672 | tf_op jit(solution)/shard_map/all_gather | solution.py:114
  191.2 32.5 %while.29 = (s32[]{:T(128)}, bf16[2,512,8,64]{1,3,2,0:T(8,128)(2,1)S(1)}, f32[2,8,512]{2,1,0:T(8,128)S(1)}, s32[2]{0:T(128)S(1)}, s32[1024]{0:T(1024)S(1)}, /*in...) while((s32[]{:T(128)}, ...), condition=%wide.region_5.6_spmd.clone, body=%wide.region_2.5_spmd.clone.sunk | while | flops 1125642240 | bytes 56250576 | solution.py:144
  193.1 4.1 fusion.117
  197.2 4.2 fusion.118
  201.5 5.9 fusion.119
  209.3 4.1 fusion.117
  213.5 4.2 fusion.118
  217.7 5.9 fusion.119
  231.3 39.2 %all_gather.65 = bf16[512,512]{1,0:T(8,128)(2,1)S(1)} all-gather(bf16[16,512]{1,0:T(8,128)(2,1)S(1)} %copy-done.44), channel_id=1, replica_groups=mesh['dp'=4,'fsdp'=8] {'dp','fsdp'}, dimensions={0}, use_global_device_ids=true | all-gather | bytes 540672 | tf_op jit(solution)/shard_map/all_gather | solution.py:115
  273.0 8.0 multiply_convert_fusion.1
  281.0 6.6 fusion.52
  294.8 6.3 convert_reduce_fusion
  313.6 93.1 %while.30 = (s32[]{:T(128)}, f32[1024,8,64]{0,2,1:T(8,128)}, f32[1024,8,64]{0,2,1:T(8,128)}, bf16[2,512,8,64]{1,3,2,0:T(8,128)(2,1)}, s32[2]{0:T(128)S(1)}, /*in...) while((s32[]{:T(128)}, f32[1024,8,64]{0,2,1:T(8,128)}, ...), condition=%wide.region_20.21_spmd.clone.clone, body=%wide.region_18.20_spmd.clone.clone.sunk | while | flops 2726555648 | bytes 188060112 | solution.py:258
  322.6 11.5 %multiply_reduce_fusion.8 = (f32[8,512]{1,0:T(8,128)}, f32[8,512,1024]{2,1,0:T(8,128)}) fusion(f32[8,512,1024]{2,1,0:T(8,128)S(1)} %fusion.129, f32[8,512]{1,0:T(8,128)} %dynamic-slice_bitcast_fusion.2, bf16[1024,8,64]{0,2,1:T(8,128)(2,1)S(1)} %get-tuple-element.634, bf16[1024,8,64]{0,2,1:T(8,128)(2,1)} %get-tuple-element.631, s32[]{:T(128)S(6)} %select_n.55, ...), kind=kOutput, calls=%fused_computation.16.clone.1 | convolution fusion | flops 557838336 | bytes 35684356 | tf_op jit(solution)/shard_map/while/body/eval_jaxpr/bhd,khd->hbk/dot_general | solution.py:65
  334.0 9.4 multiply_convert_fusion.3
  343.5 8.8 bitcast_add_fusion.5
  355.0 4.4 bitcast_add_fusion.4
  368.4 11.5 %multiply_reduce_fusion.8 = (f32[8,512]{1,0:T(8,128)}, f32[8,512,1024]{2,1,0:T(8,128)}) fusion(f32[8,512,1024]{2,1,0:T(8,128)S(1)} %fusion.129, f32[8,512]{1,0:T(8,128)} %dynamic-slice_bitcast_fusion.2, bf16[1024,8,64]{0,2,1:T(8,128)(2,1)S(1)} %get-tuple-element.634, bf16[1024,8,64]{0,2,1:T(8,128)(2,1)} %get-tuple-element.631, s32[]{:T(128)S(6)} %select_n.55, ...), kind=kOutput, calls=%fused_computation.16.clone.1 | convolution fusion | flops 557838336 | bytes 35684356 | tf_op jit(solution)/shard_map/while/body/eval_jaxpr/bhd,khd->hbk/dot_general | solution.py:65
  379.8 9.4 multiply_convert_fusion.3
  389.3 9.5 bitcast_add_fusion.5
  401.4 5.1 bitcast_add_fusion.4
  422.3 6.5 fusion.55
  430.4 6.6 fusion.46
  452.4 39.9 %all-reduce.21 = (f32[512]{0:T(512)S(1)}, f32[512]{0:T(512)S(1)}, f32[512]{0:T(512)S(1)}, f32[512]{0:T(512)S(1)}, f32[512]{0:T(512)S(1)}, /*index=5*/f32[2048]{0...) all-reduce(f32[512]{0:T(512)S(1)} %reduce_sum.243, ...), channel_id=3, replica_groups=mesh['dp'=4,'fsdp'=8] {'dp','fsdp'}, use_global_device_ids=true, to_apply=%region_23.24.clone | all-reduce | flops 6656 | bytes 53248
  497.6 81.5 %reduce-scatter.19.cloned.1.call-done = f32[16,512]{1,0:T(8,128)} async-done(((f32[512,512]{1,0:T(8,128)}), f32[16,512]{1,0:T(8,128)}) %reduce-scatter.19.cloned.1.call-update) | async-done | bytes 32784
  579.2 133.7 %reduce-scatter.21.cloned.1.call-done = f32[16,512]{1,0:T(8,128)} async-done(((f32[512,512]{1,0:T(8,128)}), f32[16,512]{1,0:T(8,128)}) %reduce-scatter.21.cloned.1.call-update) | async-done | bytes 32784
  712.8 134.0 %reduce-scatter.23.cloned.1.call-done = f32[16,512]{1,0:T(8,128)} async-done(((f32[512,512]{1,0:T(8,128)}), f32[16,512]{1,0:T(8,128)}) %reduce-scatter.23.cloned.1.call-update) | async-done | bytes 32784
  846.8 141.8 %reduce-scatter.17.cloned.1.call-done = f32[64,512]{1,0:T(8,128)} async-done(((f32[2048,512]{1,0:T(8,128)}), f32[64,512]{1,0:T(8,128)}) %reduce-scatter.17.cloned.1.call-update) | async-done | bytes 131088 | tf_op jit(solution)/shard_map/reduce_scatter | solution.py:304
  988.6 142.5 %reduce-scatter.15.cloned.1.call-done = f32[16,2048]{1,0:T(8,128)} async-done(((f32[512,2048]{1,0:T(8,128)}), f32[16,2048]{1,0:T(8,128)}) %reduce-scatter.15.cloned.1.call-update) | async-done | bytes 131088 | tf_op jit(solution)/shard_map/reduce_scatter | solution.py:303
  (298 shorter events, 105.6 us)
Async XLA Ops:
  7.2 265.8 %all-gather.3.cloned.1.call-start = ((), (), s32[]{:S(2)}) async-start(), calls=%async_computation.6 | async-start | bytes 2162688 | tf_op jit(solution)/shard_map/all_gather | solution.py:151
  7.9 273.1 %all-gather.5.cloned.1.call-start = ((), (), s32[]{:S(2)}) async-start(), calls=%async_computation.7 | async-start | bytes 2162688 | tf_op jit(solution)/shard_map/all_gather | solution.py:152
  8.7 489.0 %reduce-scatter.13.cloned.1.call-start = ((), (), s32[]{:S(2)}) async-start(), calls=%async_computation.8 | async-start | bytes 1081344 | tf_op jit(solution)/shard_map/reduce_scatter | solution.py:297
  105.0 84.3 %copy-start.23 = (bf16[512,512]{1,0:T(8,128)(2,1)}, bf16[512,512]{1,0:T(8,128)(2,1)S(1)}, u32[]{:S(2)}) copy-start(bf16[512,512]{1,0:T(8,128)(2,1)S(1)} %all_gather.60) | copy-start | bytes 1572868
  105.1 82.5 %copy-start.30 = (bf16[1024,512]{1,0:T(8,128)(2,1)S(1)}, bf16[1024,512]{1,0:T(8,128)(2,1)}, u32[]{:S(2)}) copy-start(bf16[1024,512]{1,0:T(8,128)(2,1)} %param.25) | copy-start | bytes 3145732
  144.6 40.8 %copy-start.21 = (bf16[512,512]{1,0:T(8,128)(2,1)}, bf16[512,512]{1,0:T(8,128)(2,1)S(1)}, u32[]{:S(2)}) copy-start(bf16[512,512]{1,0:T(8,128)(2,1)S(1)} %all_gather.62) | copy-start | bytes 1572868
  226.1 79.0 %copy-start.42 = (f32[512]{0:T(512)}, f32[512]{0:T(512)S(1)}, u32[]{:S(2)}) copy-start(f32[512]{0:T(512)S(1)} %convert_element_type.140) | copy-start | bytes 6148
  226.2 54.9 %copy-start.52 = (f32[512]{0:T(512)}, f32[512]{0:T(512)S(1)}, u32[]{:S(2)}) copy-start(f32[512]{0:T(512)S(1)} %convert_element_type.141) | copy-start | bytes 6148
  229.9 40.6 %copy-start.18 = (bf16[1024,512]{0,1:T(8,128)(2,1)S(1)}, bf16[1024,512]{0,1:T(8,128)(2,1)}, u32[]{:S(2)}) copy-start(bf16[1024,512]{0,1:T(8,128)(2,1)} %copy.87) | copy-start | bytes 3145732
  231.3 41.4 %copy-start.16 = (bf16[64,8,2,512]{3,1,2,0:T(8,128)(2,1)}, bf16[64,8,2,512]{3,1,2,0:T(8,128)(2,1)S(1)}, u32[]{:S(2)}) copy-start(bf16[64,8,2,512]{3,1,2,0:T(8,128)(2,1)S(1)} %copy.113) | copy-start | bytes 3145732
  272.7 32.5 %copy-start.1 = (f32[1024,512]{0,1:T(8,128)}, f32[1024,512]{0,1:T(8,128)S(1)}, u32[]{:S(2)}) copy-start(f32[1024,512]{0,1:T(8,128)S(1)} %get-tuple-element.401) | copy-start | bytes 6291460
  272.7 32.5 %copy-start.34 = (f32[1024]{0:T(1024)}, f32[1024]{0:T(1024)S(1)}, u32[]{:S(2)}) copy-start(f32[1024]{0:T(1024)S(1)} %broadcast_multiply_fusion.8) | copy-start | bytes 12292
  273.0 32.2 %copy-start.36 = (f32[1024]{0:T(1024)}, f32[1024]{0:T(1024)S(1)}, u32[]{:S(2)}) copy-start(f32[1024]{0:T(1024)S(1)} %add_rsqrt_fusion.2) | copy-start | bytes 12292
  288.9 5.9 copy-start.67
  294.7 6.4 copy-start.26
  294.8 10.4 copy-start.4
  294.8 6.3 copy-start.64
  312.4 266.7 %reduce-scatter.19.cloned.1.call-start = ((), (), s32[]{:S(2)}) async-start(), calls=%async_computation.11 | async-start | bytes 1081344
  334.0 9.4 copy-start.3
  343.5 8.9 copy-start
  343.5 8.9 copy-start.6
  355.0 4.4 copy-start.7
  379.8 9.4 copy-start.3
  389.3 9.5 copy-start
  389.3 9.5 copy-start.6
  401.4 5.1 copy-start.7
  401.4 5.1 copy-start.33
  412.5 300.3 %reduce-scatter.21.cloned.1.call-start = ((), (), s32[]{:S(2)}) async-start(), calls=%async_computation.12 | async-start | bytes 1081344
  417.3 429.5 %reduce-scatter.23.cloned.1.call-start = ((), (), s32[]{:S(2)}) async-start(), calls=%async_computation.13 | async-start | bytes 1081344
  422.2 566.4 %reduce-scatter.17.cloned.1.call-start = ((), (), s32[]{:S(2)}) async-start(), calls=%async_computation.10 | async-start | bytes 4325376 | tf_op jit(solution)/shard_map/reduce_scatter | solution.py:304
  428.9 702.2 %reduce-scatter.15.cloned.1.call-start = ((), (), s32[]{:S(2)}) async-start(), calls=%async_computation.9 | async-start | bytes 4325376 | tf_op jit(solution)/shard_map/reduce_scatter | solution.py:303
  493.0 638.6 %copy-start.66 = (f32[16]{0:T(128)}, f32[16]{0:T(128)S(1)}, u32[]{:S(2)}) copy-start(f32[16]{0:T(128)S(1)} %dynamic-slice.8) | copy-start | bytes 196
  (51 other events, 123.1 us)
Sparse Core Ops, SparseCore 0:
  11.0 59.5 all-gather.2
  73.6 55.7 all-gather.4
  312.5 132.2 reduce-scatter.12
  447.6 131.5 reduce-scatter.18
  581.8 130.9 reduce-scatter.20
  715.6 131.1 reduce-scatter.22
  849.6 138.9 reduce-scatter.16
  991.4 139.5 reduce-scatter.14
where the time goes:
time: 1140 us
  waiting for transfers between devices  635 us (56%)
  blocking collectives  245 us (21%)
  matrix products  142 us (12%)
  local copies, waits for them, and re-layouts  51.1 us (4%)
  other arithmetic  43.2 us (4%)
  between operations  15.2 us (1%)
    unnamed x11, waiting for transfers between devices  351 us
    reduce_scatter x1, waiting for transfers between devices, body(): lax.psum_scatter(up_weight_grad, ('dp', 'fsdp'), scatter_dimension=0, til...  142 us
    reduce_scatter x1, waiting for transfers between devices, body(): lax.psum_scatter(down_weight_grad, ('dp', 'fsdp'), scatter_dimension=0, t...  142 us
    unnamed x2, blocking collectives  82.2 us
    all_gather x1, blocking collectives, body(): lax.all_gather(query_weight, ('dp', 'fsdp'), axis=0, tiled=True)  43.6 us
    unnamed x170, local copies, waits for them, and re-layouts  41.3 us
    all_gather x1, blocking collectives, body(): lax.all_gather(value_weight, ('dp', 'fsdp'), axis=0, tiled=True)  40.8 us
    all_gather x1, blocking collectives, body(): lax.all_gather(key_weight, ('dp', 'fsdp'), axis=0, tiled=True)  39.5 us
  transfers between devices with their start and end apart: 8, of which 5 were waited for; matrix products, arithmetic and copies ran while one was open for 17% of the time, Pallas kernels for 0%

commit v1 on v0

--- a/solution.py
+++ b/solution.py
@@ -1,3 +1,4 @@
+import functools
 import math
 
 import jax
@@ -66,7 +67,113 @@
     return (jnp.where(visible[None], scores, neg_large), chosen)
 
 
+AXES = ("dp", "fsdp")
+
+
+def radices(extent):
+    found = []
+    while extent > 1:
+        found.append(4 if extent % 4 == 0 else 2)
+        extent //= found[-1]
+    return found
+
+
+class Links:
+    def __init__(self, mesh):
+        self.dp, self.fsdp = mesh.shape["dp"], mesh.shape["fsdp"]
+        self.count = self.dp * self.fsdp
+        self.z = self.fsdp // 2
+
+    def flat(self):
+        return lax.axis_index("dp") * self.fsdp + lax.axis_index("fsdp")
+
+    def swap(self, values, distance):
+        return lax.ppermute(values, AXES, [(i, i ^ distance) for i in range(self.count)])
+
+    def digits(self, shift, extent):
+        found = []
+        for radix in radices(extent):
+            found.append((shift, radix))
+            shift += radix.bit_length() - 1
+        return found
+
+    def stages(self):
+        z_bits = self.z.bit_length() - 1
+        return self.digits(1, self.z), self.digits(1 + z_bits, self.dp)
+
+    def gather(self, block):
+        me = self.flat()
+        shape = block.shape
+        for shift, radix in sum(self.stages(), []):
+            digit = (me >> shift) & (radix - 1)
+            parts = [block] + [self.swap(block, k << shift) for k in range(1, radix)]
+            whole = jnp.zeros((radix,) + block.shape, block.dtype)
+            for k, part in enumerate(parts):
+                whole = lax.dynamic_update_index_in_dim(whole, part, digit ^ k, 0)
+            block = whole.reshape((-1,) + shape)
+        other = self.swap(block, 1)
+        even = (me & 1) == 0
+        pair = jnp.stack([jnp.where(even, block, other), jnp.where(even, other, block)], axis=1)
+        return pair.reshape((self.count,) + shape)
+
+    def scatter(self, blocks):
+        me = self.flat()
+        shape = blocks.shape[1:]
+        core = me & 1
+        pairs = blocks.reshape((self.count // 2, 2) + shape)
+        away = lax.dynamic_index_in_dim(pairs, 1 - core, 1, keepdims=False).astype(jnp.bfloat16)
+        total = lax.dynamic_index_in_dim(pairs, core, 1, keepdims=False)
+        total = total + self.swap(away, 1).astype(jnp.float32)
+        for shift, radix in reversed(sum(self.stages(), [])):
+            digit = (me >> shift) & (radix - 1)
+            total = total.reshape((radix, -1) + shape)
+            kept = lax.dynamic_index_in_dim(total, digit, 0, keepdims=False)
+            for k in range(1, radix):
+                away = lax.dynamic_index_in_dim(total, digit ^ k, 0, keepdims=False)
+                kept = kept + self.swap(away.astype(jnp.bfloat16), k << shift).astype(jnp.float32)
+            total = kept
+        return total.reshape(shape)
+
+
+def gather_all(links, weights, vectors):
+    width = weights[0].shape[1]
+    lengths = [array.shape[0] for array in weights]
+    pieces = list(weights)
+    if vectors:
+        line = jnp.concatenate(vectors)
+        pieces.append(jnp.zeros((8, width), line.dtype).at[0, : line.shape[0]].set(line))
+    whole = links.gather(jnp.concatenate(pieces, axis=0))
+    found, at = [], 0
+    for length in lengths:
+        found.append(whole[:, at : at + length].reshape(-1, width))
+        at += length
+    lines, place = [], 0
+    for vector in vectors:
+        size = vector.shape[0]
+        lines.append(whole[:, at, place : place + size].reshape(-1))
+        place += size
+    return found, lines
+
+
+def scatter_all(links, weights, vectors):
+    count, _, width = weights[0].shape
+    line = jnp.concatenate([vector.reshape(count, -1) for vector in vectors], axis=1)
+    tail = jnp.pad(line[:, None], ((0, 0), (0, 7), (0, width - line.shape[1])))
+    total = links.scatter(jnp.concatenate(list(weights) + [tail], axis=1))
+    found, at = [], 0
+    for array in weights:
+        found.append(total[at : at + array.shape[1]])
+        at += array.shape[1]
+    lines, place = [], 0
+    for vector in vectors:
+        size = vector.shape[0] // count
+        lines.append(total[at, place : place + size])
+        place += size
+    return found, lines
+
+
 def body(
+    links,
     stream_x,
     stream_y,
     cotangent,
@@ -98,26 +205,40 @@
     bounds = jnp.cumsum(doc_lengths[0])
     position = jnp.arange(length, dtype=jnp.int32)
     segment = jnp.sum((position[:, None] >= bounds[None, :]).astype(jnp.int32), axis=1)
-    (
-        whole_query,
-        whole_key,
-        whole_value,
-        whole_output,
+    rows = query_weight.shape[0]
+    count = links.count
+    vectors = [
+        query_bias,
+        value_bias,
+        output_bias,
+        first_gain,
+        first_shift,
+        down_bias,
+        second_gain,
+        second_shift,
+        final_gain,
+        final_shift,
+        up_bias,
+    ]
+    near = gather_all(links, [query_weight, key_weight, value_weight], vectors)
+    (whole_query, whole_key, whole_value), (
         bias_query,
         bias_value,
         bias_output,
         gain_first,
         shift_first,
-    ) = (
-        lax.all_gather(query_weight, ("dp", "fsdp"), axis=0, tiled=True),
-        lax.all_gather(key_weight, ("dp", "fsdp"), axis=0, tiled=True),
-        lax.all_gather(value_weight, ("dp", "fsdp"), axis=0, tiled=True),
-        lax.all_gather(output_weight, ("dp", "fsdp"), axis=0, tiled=True),
-        lax.all_gather(query_bias, ("dp", "fsdp"), axis=0, tiled=True),
-        lax.all_gather(value_bias, ("dp", "fsdp"), axis=0, tiled=True),
-        lax.all_gather(output_bias, ("dp", "fsdp"), axis=0, tiled=True),
-        lax.all_gather(first_gain, ("dp", "fsdp"), axis=0, tiled=True),
-        lax.all_gather(first_shift, ("dp", "fsdp"), axis=0, tiled=True),
+        bias_down,
+        gain_second,
+        shift_second,
+        gain_final,
+        shift_final,
+        bias_up,
+    ) = near
+    columns = up_weight.shape[1] // width
+    apart = up_weight.reshape(rows, columns, width).swapaxes(0, 1).reshape(-1, width)
+    (whole_output, whole_up, whole_down), _ = gather_all(links, [output_weight, apart, down_weight], [])
+    whole_up = (
+        whole_up.reshape(count, columns, rows, width).swapaxes(1, 2).reshape(width, columns * width)
     )
     queries = (
         (project(stream_x, whole_query) + bias_query)
@@ -147,16 +268,6 @@
     first_normed, first_scale = normalize(stream_x.astype(jnp.float32) + branch)
     first_out = first_normed * gain_first + shift_first
     mid_y = stream_y.astype(jnp.float32) + branch
-    whole_up, whole_down, bias_up, bias_down, gain_second, shift_second, gain_final, shift_final = (
-        lax.all_gather(up_weight, ("dp", "fsdp"), axis=0, tiled=True),
-        lax.all_gather(down_weight, ("dp", "fsdp"), axis=0, tiled=True),
-        lax.all_gather(up_bias, ("dp", "fsdp"), axis=0, tiled=True),
-        lax.all_gather(down_bias, ("dp", "fsdp"), axis=0, tiled=True),
-        lax.all_gather(second_gain, ("dp", "fsdp"), axis=0, tiled=True),
-        lax.all_gather(second_shift, ("dp", "fsdp"), axis=0, tiled=True),
-        lax.all_gather(final_gain, ("dp", "fsdp"), axis=0, tiled=True),
-        lax.all_gather(final_shift, ("dp", "fsdp"), axis=0, tiled=True),
-    )
     first_low = first_out.astype(jnp.bfloat16)
     hidden_pre = project(first_low, whole_up) + bias_up
     hidden = gelu_exact(hidden_pre).astype(jnp.bfloat16)
@@ -167,16 +278,6 @@
     block_out = (
         second_normed * gain_second + shift_second + final_normed * gain_final + shift_final
     ).astype(jnp.bfloat16)
-    whole_up, whole_down, bias_up, bias_down, gain_second, shift_second, gain_final, shift_final = (
-        lax.all_gather(up_weight, ("dp", "fsdp"), axis=0, tiled=True),
-        lax.all_gather(down_weight, ("dp", "fsdp"), axis=0, tiled=True),
-        lax.all_gather(up_bias, ("dp", "fsdp"), axis=0, tiled=True),
-        lax.all_gather(down_bias, ("dp", "fsdp"), axis=0, tiled=True),
-        lax.all_gather(second_gain, ("dp", "fsdp"), axis=0, tiled=True),
-        lax.all_gather(second_shift, ("dp", "fsdp"), axis=0, tiled=True),
-        lax.all_gather(final_gain, ("dp", "fsdp"), axis=0, tiled=True),
-        lax.all_gather(final_shift, ("dp", "fsdp"), axis=0, tiled=True),
-    )
     upstream = cotangent.astype(jnp.float32)
     final_gain_grad = jnp.sum(upstream * final_normed, axis=0)
     final_shift_grad = jnp.sum(upstream, axis=0)
@@ -192,27 +293,6 @@
     up_bias_grad = column_sum(hidden_grad)
     up_weight_grad = outer_sum(first_low, hidden_grad)
     first_grad = second_back + project_back(hidden_grad, whole_up)
-    (
-        whole_query,
-        whole_key,
-        whole_value,
-        whole_output,
-        bias_query,
-        bias_value,
-        bias_output,
-        gain_first,
-        shift_first,
-    ) = (
-        lax.all_gather(query_weight, ("dp", "fsdp"), axis=0, tiled=True),
-        lax.all_gather(key_weight, ("dp", "fsdp"), axis=0, tiled=True),
-        lax.all_gather(value_weight, ("dp", "fsdp"), axis=0, tiled=True),
-        lax.all_gather(output_weight, ("dp", "fsdp"), axis=0, tiled=True),
-        lax.all_gather(query_bias, ("dp", "fsdp"), axis=0, tiled=True),
-        lax.all_gather(value_bias, ("dp", "fsdp"), axis=0, tiled=True),
-        lax.all_gather(output_bias, ("dp", "fsdp"), axis=0, tiled=True),
-        lax.all_gather(first_gain, ("dp", "fsdp"), axis=0, tiled=True),
-        lax.all_gather(first_shift, ("dp", "fsdp"), axis=0, tiled=True),
-    )
     first_gain_grad = jnp.sum(first_grad * first_normed, axis=0)
     first_shift_grad = jnp.sum(first_grad, axis=0)
     first_back = norm_back(first_grad * gain_first, first_normed, first_scale)
@@ -272,42 +352,46 @@
         + project_back(key_grad, whole_key)
         + project_back(value_grad, whole_value)
     )
-    (
-        query_weight_share,
-        key_weight_share,
-        value_weight_share,
-        output_weight_share,
-        query_bias_share,
-        value_bias_share,
+    rows = query_weight.shape[0]
+    count = links.count
+
+    def split_rows(grad):
+        return grad.reshape(count, rows, -1, width).swapaxes(1, 2).reshape(count, -1, width)
+
+    small = [
+        output_bias_grad,
+        first_gain_grad,
+        first_shift_grad,
+        down_bias_grad,
+        second_gain_grad,
+        final_shift_grad,
+        final_gain_grad,
+        up_bias_grad,
+    ]
+    later = scatter_all(
+        links,
+        [split_rows(output_weight_grad), split_rows(up_weight_grad), down_weight_grad.reshape(count, -1, width)],
+        small,
+    )
+    (output_weight_share, up_weight_share, down_weight_share), (
         output_bias_share,
         first_gain_share,
         first_shift_share,
-        up_weight_share,
-        down_weight_share,
-        up_bias_share,
         down_bias_share,
         second_gain_share,
         second_shift_share,
         final_gain_share,
-        final_shift_share,
-    ) = (
-        lax.psum_scatter(query_weight_grad, ("dp", "fsdp"), scatter_dimension=0, tiled=True),
-        lax.psum_scatter(key_weight_grad, ("dp", "fsdp"), scatter_dimension=0, tiled=True),
-        lax.psum_scatter(value_weight_grad, ("dp", "fsdp"), scatter_dimension=0, tiled=True),
-        lax.psum_scatter(output_weight_grad, ("dp", "fsdp"), scatter_dimension=0, tiled=True),
-        lax.psum_scatter(query_bias_grad, ("dp", "fsdp"), scatter_dimension=0, tiled=True),
-        lax.psum_scatter(value_bias_grad, ("dp", "fsdp"), scatter_dimension=0, tiled=True),
-        lax.psum_scatter(output_bias_grad, ("dp", "fsdp"), scatter_dimension=0, tiled=True),
-        lax.psum_scatter(first_gain_grad, ("dp", "fsdp"), scatter_dimension=0, tiled=True),
-        lax.psum_scatter(first_shift_grad, ("dp", "fsdp"), scatter_dimension=0, tiled=True),
-        lax.psum_scatter(up_weight_grad, ("dp", "fsdp"), scatter_dimension=0, tiled=True),
-        lax.psum_scatter(down_weight_grad, ("dp", "fsdp"), scatter_dimension=0, tiled=True),
-        lax.psum_scatter(up_bias_grad, ("dp", "fsdp"), scatter_dimension=0, tiled=True),
-        lax.psum_scatter(down_bias_grad, ("dp", "fsdp"), scatter_dimension=0, tiled=True),
-        lax.psum_scatter(second_gain_grad, ("dp", "fsdp"), scatter_dimension=0, tiled=True),
-        lax.psum_scatter(final_shift_grad, ("dp", "fsdp"), scatter_dimension=0, tiled=True),
-        lax.psum_scatter(final_gain_grad, ("dp", "fsdp"), scatter_dimension=0, tiled=True),
-        lax.psum_scatter(final_shift_grad, ("dp", "fsdp"), scatter_dimension=0, tiled=True),
+        up_bias_share,
+    ) = later
+    final_shift_share = second_shift_share
+    up_weight_share = up_weight_share.reshape(-1, rows, width).swapaxes(0, 1).reshape(rows, -1)
+    (query_weight_share, key_weight_share, value_weight_share), (
+        query_bias_share,
+        value_bias_share,
+    ) = scatter_all(
+        links,
+        [split_rows(query_weight_grad), split_rows(key_weight_grad), split_rows(value_weight_grad)],
+        [query_bias_grad, value_bias_grad],
     )
     return (
         block_out,
@@ -358,7 +442,7 @@
         P(("dp", "fsdp")),
     )
     return jax.shard_map(
-        body,
+        functools.partial(body, Links(mesh)),
         mesh=mesh,
         in_specs=placed,
         out_specs=(

time: 1140 us -> 409 us (0.36)
  waiting for transfers between devices: 635 us -> 60.7 us
  blocking collectives: 245 us -> 0 us
  starting transfers between devices: 0.32 us -> 35.9 us
  local copies, waits for them, and re-layouts: 51.1 us -> 71.8 us
  other arithmetic: 43.2 us -> 63.8 us
  matrix products: 142 us -> 161 us
  between operations: 15.2 us -> 2.23 us
    unnamed x11 -> x0, waiting for transfers between devices: 351 us -> none
    reduce_scatter x3 -> x0, waiting for transfers between devices: 284 us -> none  [the longest x1 142 us: body(): lax.psum_scatter(up_weight_grad, ('dp', 'fsdp'), scatter_dimension=0, til...]
    all_gather x4 -> x0, blocking collectives: 163 us -> none  [the longest x1 43.6 us: body(): lax.all_gather(query_weight, ('dp', 'fsdp'), axis=0, tiled=True)]
    unnamed x2 -> x0, blocking collectives: 82.2 us -> none
    ppermute x0 -> x28, waiting for transfers between devices: none -> 60.7 us  [swap(): lax.ppermute(values, AXES, [(i, i ^ distance) for i in range(self.count)])]
    ppermute x0 -> x28, starting transfers between devices: none -> 35.9 us  [swap(): lax.ppermute(values, AXES, [(i, i ^ distance) for i in range(self.count)])]
    unnamed x170 -> x124, local copies, waits for them, and re-layouts: 41.3 us -> 22.1 us
    reshape x0 -> x14, local copies, waits for them, and re-layouts: none -> 14.4 us  [the longest x2 12.1 us: split_rows(): grad.reshape(count, rows, -1, width).swapaxes(1, 2)]
  transfers between devices with their start and end apart: 8 -> 28, of which waited for: 5 -> 13; matrix products, arithmetic and copies ran while one was open for 17% -> 53% of each run, Pallas kernels for 0% -> 0%
where the time goes in v1:
time: 409 us; the launch traced here: 403 us
  matrix products  161 us (39%)
  local copies, waits for them, and re-layouts  71.8 us (18%)
  other arithmetic  63.8 us (16%)
  waiting for transfers between devices  60.7 us (15%)
  starting transfers between devices  35.9 us (9%)
  loops' own time  7.56 us (2%)
    ppermute x28, waiting for transfers between devices, swap(): lax.ppermute(values, AXES, [(i, i ^ distance) for i in range(self.count)])  60.7 us
    dot_general x4, matrix products, block_scores(): jnp.einsum('bhd,khd->hbk', chosen, keys, preferred_element_type=jnp.float32)  40.4 us
    ppermute x28, starting transfers between devices, swap(): lax.ppermute(values, AXES, [(i, i ^ distance) for i in range(self.count)])  35.9 us
    unnamed x124, local copies, waits for them, and re-layouts  22.1 us
    dot_general x2, matrix products, attend_back(): jnp.einsum('bhd,khd->hbk', incoming, values, preferred_element_type=jnp.f...  19 us
    dot_general x6, matrix products, project_back(): jnp.einsum('te,de->td', gradients, weight, preferred_element_type=jnp.flo...  18.9 us
    dot_general x6, matrix products, project(): return jnp.dot(inputs, weight, preferred_element_type=jnp.float32)  18.8 us
    convert_element_type x2, other arithmetic, attend_back(): score_grad = (attention * (weight_grad - balance)).astype(jnp.bfloat16)  18.7 us
  transfers between devices with their start and end apart: 28, of which 13 were waited for; matrix products, arithmetic and copies ran while one was open for 53% of the time, Pallas kernels for 0%

profile of v1, /device:TPU:0, one launch (start us, length us, event | category | flops | bytes accessed | tf_op | source)
XLA Modules:
  0.0 402.9 jit_solution(4817801329942565673)
XLA Ops:
  8.1 7.4 %concatenate.39 = bf16[224]{0:T(256)(128)(2,1)S(1)} concatenate(bf16[16]{0:T(256)(128)(2,1)} %param.32, bf16[16]{0:T(256)(128)(2,1)} %param.35, bf16[16]{0:T(256)(128)(2,1)} %param.37, bf16[16]{0:T(256)(128)(2,1)} %param.38, bf16[16]{0:T(256)(128)(2,1)} %param.39, bf16[16]{0:T(256)(128)(2,1)} %param.43, bf16[16]{0:T(256)(128)(2,1)} %param.44, bf16[16]{0:T(256)(128)(2,1)} %param.45, ...), dimensions={0} | concatenate | bytes 896 | tf_op jit(solution)/shard_map/concatenate | solution.py:143
  27.1 5.9 %collective-permute-done.2 = bf16[56,512]{1,0:T(8,128)(2,1)S(1)} collective-permute-done((bf16[56,512]{1,0:T(8,128)(2,1)S(1)}, bf16[56,512]{1,0:T(8,128)(2,1)S(1)}, u32[]{:S(2)}, u32[]{:S(2)}) %collective-permute-start.2) | collective-permute-done | bytes 57376 | tf_op jit(solution)/shard_map/ppermute | solution.py:91
  50.1 9.1 %collective-permute-done.10 = bf16[4,144,512]{2,1,0:T(8,128)(2,1)S(1)} collective-permute-done((bf16[4,144,512]{2,1,0:T(8,128)(2,1)S(1)}, bf16[4,144,512]{2,1,0:T(8,128)(2,1)S(1)}, u32[]{:S(2)}, u32[]{:S(2)}) %collective-permute-start.10) | collective-permute-done | bytes 589856 | tf_op jit(solution)/shard_map/ppermute | solution.py:91
  60.0 9.5 %collective-permute-done.11 = bf16[4,144,512]{2,1,0:T(8,128)(2,1)S(1)} collective-permute-done((bf16[4,144,512]{2,1,0:T(8,128)(2,1)S(1)}, bf16[4,144,512]{2,1,0:T(8,128)(2,1)S(1)}, u32[]{:S(2)}, u32[]{:S(2)}) %collective-permute-start.11) | collective-permute-done | bytes 589856 | tf_op jit(solution)/shard_map/ppermute | solution.py:91
  81.1 34.1 %while.30 = (s32[]{:T(128)}, bf16[2,512,8,64]{1,3,2,0:T(8,128)(2,1)S(1)}, f32[2,8,512]{2,1,0:T(8,128)}, s32[2]{0:T(128)S(1)}, s32[1024]{0:T(1024)S(1)}, /*index=...) while((s32[]{:T(128)}, ...), condition=%wide.region_5.6_spmd.clone, body=%wide.region_2.0_spmd.clone.sunk | while | flops 1125642240 | bytes 56251076 | solution.py:265
  92.2 5.9 %fusion.149 = bf16[2,512,8,64]{1,3,2,0:T(8,128)(2,1)S(1)} fusion(bf16[2,512,8,64]{1,3,2,0:T(8,128)(2,1)S(1)} %get-tuple-element.583, s32[]{:T(128)} %get-tuple-element.582, bf16[1024,8,64]{0,2,1:T(8,128)(2,1)} %get-tuple-element.603, f32[8,512,1024]{2,1,0:T(8,128)S(1)} %get-tuple-element.553, f32[8,512]{1,0:T(8,128)S(1)} %fusion.148, ...), kind=kOutput, calls=%fused_computation.8.clone.1 | convolution fusion | flops 557842432 | bytes 19431428 | tf_op jit(solution)/shard_map/while/body/eval_jaxpr/hbk,khd->bhd/dot_general | solution.py:262
  109.0 5.9 %fusion.149 = bf16[2,512,8,64]{1,3,2,0:T(8,128)(2,1)S(1)} fusion(bf16[2,512,8,64]{1,3,2,0:T(8,128)(2,1)S(1)} %get-tuple-element.583, s32[]{:T(128)} %get-tuple-element.582, bf16[1024,8,64]{0,2,1:T(8,128)(2,1)} %get-tuple-element.603, f32[8,512,1024]{2,1,0:T(8,128)S(1)} %get-tuple-element.553, f32[8,512]{1,0:T(8,128)S(1)} %fusion.148, ...), kind=kOutput, calls=%fused_computation.8.clone.1 | convolution fusion | flops 557842432 | bytes 19431428 | tf_op jit(solution)/shard_map/while/body/eval_jaxpr/hbk,khd->bhd/dot_general | solution.py:262
  127.5 5.6 %multiply_convert_fusion.1 = (bf16[1024,2048]{1,0:T(8,128)(2,1)}, f32[1024,2048]{1,0:T(8,128)S(1)}) fusion(f32[2048]{0:T(1024)S(1)} %reshape.590, bf16[512,2048]{1,0:T(8,128)(2,1)S(1)} %bitcast.309, f32[1024,512]{0,1:T(8,128)S(1)} %get-tuple-element.382, f32[512]{0:T(512)S(1)} %reshape.589, f32[512]{0:T(512)S(1)} %reshape.588, ...), kind=kOutput, calls=%fused_computation.45 | convolution fusion | flops 2162688000 | bytes 16797696 | tf_op jit(solution)/shard_map/dot_general | solution.py:44
  133.1 5.6 %fusion.79 = (f32[1024]{0:T(1024)S(1)}, f32[1024,512]{0,1:T(8,128)S(1)}, f32[1024]{0:T(1024)S(1)}, f32[1024,512]{0,1:T(8,128)S(1)}) fusion(f32[512]{0:T(512)S(1)} %reshape.591, f32[1024,512]{0,1:T(8,128)S(1)} %get-tuple-element.425, f32[512]{0:T(512)S(1)} %reshape.587, bf16[1024,512]{0,1:T(8,128)(2,1)S(1)} %copy-done.34, f32[512]{0:T(512)S(1)} %reshape.589, ...), kind=kOutput, calls=%fused_computation.211 | convolution fusion | flops 2153773056 | bytes 15753216 | tf_op jit(solution)/shard_map/dot_general | solution.py:44
  144.8 4.4 %fusion.86 = f32[2048,512]{1,0:T(8,128)} fusion(bf16[1024,2048]{1,0:T(8,128)(2,1)S(1)} %copy-done.59, bf16[1024,512]{0,1:T(8,128)(2,1)S(1)} %get-tuple-element.371), kind=kOutput, calls=%fused_computation.218 | convolution fusion | flops 2147483648 | bytes 9437184 | tf_op jit(solution)/shard_map/td,te->de/dot_general | solution.py:52
  149.2 5.9 %convert_reduce_fusion = (f32[2048]{0:T(1024)S(1)}, bf16[1024,2048]{1,0:T(8,128)(2,1)S(1)}) fusion(f32[1024,2048]{1,0:T(8,128)S(1)} %get-tuple-element.427, f32[2048]{0:T(1024)S(1)} %reshape.590, bf16[1024,512]{0,1:T(8,128)(2,1)S(1)} %get-tuple-element.371, bf16[2048,512]{1,0:T(8,128)(2,1)S(1)} %bitcast.318), kind=kOutput, calls=%fused_computation.44 | convolution fusion | flops 2174744576 | bytes 15745024 | tf_op jit(solution)/shard_map/te,de->td/dot_general | solution.py:48
  155.1 4.5 %fusion.73 = f32[512,2048]{1,0:T(8,128)} fusion(bf16[1024,2048]{1,0:T(8,128)(2,1)S(1)} %get-tuple-element.430, f32[1024,512]{0,1:T(8,128)S(1)} %get-tuple-element.382, f32[512]{0:T(512)S(1)} %reshape.589, f32[512]{0:T(512)S(1)} %reshape.588, f32[1024]{0:T(1024)S(1)} %add_rsqrt_fusion.2, f32[1024]{0:T(1024)S(1)} %broadcast_multiply_fusion.8), kind=kOutput, calls=%fused_computation.208 | convolution fusion | flops 2150105088 | bytes 10498048 | tf_op jit(solution)/shard_map/td,te->de/dot_general | solution.py:52
  159.6 4.6 %multiply_reduce_fusion.1 = (f32[512]{0:T(512)S(1)}, f32[1024]{0:T(1024)S(1)}, f32[1024]{0:T(1024)S(1)}, f32[512]{0:T(512)S(1)}, f32[1024,512]{0,1:T(8,128)}) fusion(f32[1024,512]{0,1:T(8,128)S(1)} %get-tuple-element.382, f32[1024]{0:T(1024)S(1)} %add_rsqrt_fusion.2, f32[1024]{0:T(1024)S(1)} %broadcast_multiply_fusion.8, f32[512]{0:T(512)S(1)} %reshape.588, ...), kind=kOutput, calls=%fused_computation.74 | convolution fusion | flops 2156917760 | bytes 13672448 | tf_op jit(solution)/shard_map/te,de->td/dot_general | solution.py:48
  164.2 6.0 %reshape.572 = f32[32,16,4,512]{3,2,1,0:T(4,128)} reshape(f32[512,2048]{1,0:T(8,128)} %fusion.73) | data formatting | bytes 8388608 | tf_op jit(solution)/shard_map/reshape | solution.py:359
  170.2 6.1 %copy.92 = f32[32,16,4,512]{3,1,2,0:T(8,128)} copy(f32[32,16,4,512]{3,2,1,0:T(4,128)} %reshape.572) | data formatting | bytes 8388608 | tf_op jit(solution)/shard_map/reshape | solution.py:359
  193.6 119.3 %while.31 = (s32[]{:T(128)}, f32[1024,8,64]{0,2,1:T(8,128)}, f32[1024,8,64]{0,2,1:T(8,128)}, bf16[2,512,8,64]{1,3,2,0:T(8,128)(2,1)}, s32[2]{0:T(128)S(1)}, /*in...) while((s32[]{:T(128)}, f32[1024,8,64]{0,2,1:T(8,128)}, ...), condition=%wide.region_20.21_spmd.clone.clone, body=%wide.region_18.20_spmd.clone.clone.sunk | while | flops 2726555648 | bytes 267489744 | solution.py:338
  196.5 9.5 %fusion.159 = f32[8,512,1024]{2,1,0:T(8,128)} fusion(bf16[1024,8,64]{0,2,1:T(8,128)(2,1)} %get-tuple-element.653, bf16[1024,8,64]{0,2,1:T(8,128)(2,1)} %get-tuple-element.652, s32[]{:T(128)S(6)} %select_n.169), kind=kOutput, calls=%fused_computation.27.clone.1 | convolution fusion | flops 536870912 | bytes 18350084 | tf_op jit(solution)/shard_map/while/body/eval_jaxpr/bhd,khd->hbk/dot_general | solution.py:315
  209.3 16.0 %multiply_reduce_fusion.8 = (f32[8,512]{1,0:T(8,128)}, f32[8,512,1024]{2,1,0:T(8,128)}) fusion(f32[8,512,1024]{2,1,0:T(8,128)} %fusion.159, f32[8,512]{1,0:T(8,128)} %dynamic-slice_bitcast_fusion.2, bf16[1024,8,64]{0,2,1:T(8,128)(2,1)S(1)} %get-tuple-element.650, bf16[1024,8,64]{0,2,1:T(8,128)(2,1)} %get-tuple-element.647, s32[]{:T(128)S(6)} %select_n.169, ...), kind=kOutput, calls=%fused_computation.16.clone.1 | convolution fusion | flops 557838336 | bytes 35684356 | tf_op jit(solution)/shard_map/while/body/eval_jaxpr/bhd,khd->hbk/dot_general | solution.py:66
  225.4 9.3 %multiply_convert_fusion.3 = bf16[8,512,1024]{2,1,0:T(8,128)(2,1)} fusion(f32[8,512,1024]{2,1,0:T(8,128)} %get-tuple-element.567, f32[8,512,1024]{2,1,0:T(8,128)S(1)} %bitcast.281, f32[8,512]{1,0:T(8,128)} %get-tuple-element.568), kind=kLoop, calls=%fused_computation.15.clone.1 | loop fusion | flops 12582912 | bytes 41959424 | tf_op jit(solution)/shard_map/while/body/eval_jaxpr/convert_element_type | solution.py:319
  234.7 6.6 %bitcast_add_fusion.8 = f32[1024,8,64]{0,2,1:T(8,128)} fusion(f32[1024,8,64]{0,2,1:T(8,128)} %get-tuple-element.626, bf16[8,512,1024]{2,1,0:T(8,128)(2,1)} %multiply_convert_fusion.3, pred[]{:T(512)S(6)} %compare.19, bf16[1024,8,64]{0,2,1:T(8,128)(2,1)} %get-tuple-element.647, s32[]{:T(128)S(6)} %select_n.169), kind=kOutput, calls=%fused_computation.21.clone.1 | convolution fusion | flops 538443776 | bytes 13107205 | tf_op jit(solution)/shard_map/while/body/eval_jaxpr/hbk,bhd->khd/dot_general | solution.py:326
  241.3 6.9 %fusion.160 = bf16[2,512,8,64]{1,3,2,0:T(8,128)(2,1)S(1)} fusion(bf16[2,512,8,64]{1,3,2,0:T(8,128)(2,1)S(1)} %copy-done.12, s32[]{:T(128)} %get-tuple-element.625, bf16[8,512,1024]{2,1,0:T(8,128)(2,1)} %multiply_convert_fusion.3, bf16[1024,8,64]{0,2,1:T(8,128)(2,1)S(1)} %get-tuple-element.650), kind=kOutput, calls=%fused_computation.25.clone.1 | convolution fusion | flops 537133056 | bytes 10485764 | tf_op jit(solution)/shard_map/while/body/eval_jaxpr/hbk,khd->bhd/dot_general | solution.py:321
  248.2 4.5 %bitcast_add_fusion.9 = f32[1024,8,64]{0,2,1:T(8,128)} fusion(f32[1024,8,64]{0,2,1:T(8,128)} %get-tuple-element.627, f32[8,512,1024]{2,1,0:T(8,128)S(1)} %copy-done, pred[]{:T(512)S(6)} %compare.19, bf16[1024,8,64]{0,2,1:T(8,128)(2,1)} %get-tuple-element.652, s32[]{:T(128)S(6)} %select_n.169), kind=kOutput, calls=%fused_computation.20.clone.1 | convolution fusion | flops 542113792 | bytes 21495812 | tf_op jit(solution)/shard_map/while/body/eval_jaxpr/hbk,bhd->khd/dot_general | solution.py:329
  255.3 9.5 %fusion.159 = f32[8,512,1024]{2,1,0:T(8,128)} fusion(bf16[1024,8,64]{0,2,1:T(8,128)(2,1)} %get-tuple-element.653, bf16[1024,8,64]{0,2,1:T(8,128)(2,1)} %get-tuple-element.652, s32[]{:T(128)S(6)} %select_n.169), kind=kOutput, calls=%fused_computation.27.clone.1 | convolution fusion | flops 536870912 | bytes 18350084 | tf_op jit(solution)/shard_map/while/body/eval_jaxpr/bhd,khd->hbk/dot_general | solution.py:315
  268.1 16.0 %multiply_reduce_fusion.8 = (f32[8,512]{1,0:T(8,128)}, f32[8,512,1024]{2,1,0:T(8,128)}) fusion(f32[8,512,1024]{2,1,0:T(8,128)} %fusion.159, f32[8,512]{1,0:T(8,128)} %dynamic-slice_bitcast_fusion.2, bf16[1024,8,64]{0,2,1:T(8,128)(2,1)S(1)} %get-tuple-element.650, bf16[1024,8,64]{0,2,1:T(8,128)(2,1)} %get-tuple-element.647, s32[]{:T(128)S(6)} %select_n.169, ...), kind=kOutput, calls=%fused_computation.16.clone.1 | convolution fusion | flops 557838336 | bytes 35684356 | tf_op jit(solution)/shard_map/while/body/eval_jaxpr/bhd,khd->hbk/dot_general | solution.py:66
  284.2 9.3 %multiply_convert_fusion.3 = bf16[8,512,1024]{2,1,0:T(8,128)(2,1)} fusion(f32[8,512,1024]{2,1,0:T(8,128)} %get-tuple-element.567, f32[8,512,1024]{2,1,0:T(8,128)S(1)} %bitcast.281, f32[8,512]{1,0:T(8,128)} %get-tuple-element.568), kind=kLoop, calls=%fused_computation.15.clone.1 | loop fusion | flops 12582912 | bytes 41959424 | tf_op jit(solution)/shard_map/while/body/eval_jaxpr/convert_element_type | solution.py:319
  293.5 7.2 %bitcast_add_fusion.8 = f32[1024,8,64]{0,2,1:T(8,128)} fusion(f32[1024,8,64]{0,2,1:T(8,128)} %get-tuple-element.626, bf16[8,512,1024]{2,1,0:T(8,128)(2,1)} %multiply_convert_fusion.3, pred[]{:T(512)S(6)} %compare.19, bf16[1024,8,64]{0,2,1:T(8,128)(2,1)} %get-tuple-element.647, s32[]{:T(128)S(6)} %select_n.169), kind=kOutput, calls=%fused_computation.21.clone.1 | convolution fusion | flops 538443776 | bytes 13107205 | tf_op jit(solution)/shard_map/while/body/eval_jaxpr/hbk,bhd->khd/dot_general | solution.py:326
  300.7 6.9 %fusion.160 = bf16[2,512,8,64]{1,3,2,0:T(8,128)(2,1)S(1)} fusion(bf16[2,512,8,64]{1,3,2,0:T(8,128)(2,1)S(1)} %copy-done.12, s32[]{:T(128)} %get-tuple-element.625, bf16[8,512,1024]{2,1,0:T(8,128)(2,1)} %multiply_convert_fusion.3, bf16[1024,8,64]{0,2,1:T(8,128)(2,1)S(1)} %get-tuple-element.650), kind=kOutput, calls=%fused_computation.25.clone.1 | convolution fusion | flops 537133056 | bytes 10485764 | tf_op jit(solution)/shard_map/while/body/eval_jaxpr/hbk,khd->bhd/dot_general | solution.py:321
  307.6 5.2 %bitcast_add_fusion.9 = f32[1024,8,64]{0,2,1:T(8,128)} fusion(f32[1024,8,64]{0,2,1:T(8,128)} %get-tuple-element.627, f32[8,512,1024]{2,1,0:T(8,128)S(1)} %copy-done, pred[]{:T(512)S(6)} %compare.19, bf16[1024,8,64]{0,2,1:T(8,128)(2,1)} %get-tuple-element.652, s32[]{:T(128)S(6)} %select_n.169), kind=kOutput, calls=%fused_computation.20.clone.1 | convolution fusion | flops 542113792 | bytes 21495812 | tf_op jit(solution)/shard_map/while/body/eval_jaxpr/hbk,bhd->khd/dot_general | solution.py:329
  336.1 4.2 %collective-permute-done.15 = bf16[4,56,512]{2,1,0:T(8,128)(2,1)S(1)} collective-permute-done((bf16[4,56,512]{2,1,0:T(8,128)(2,1)S(1)}, bf16[4,56,512]{2,1,0:T(8,128)(2,1)S(1)}, u32[]{:S(2)}, u32[]{:S(2)}) %collective-permute-start.15) | collective-permute-done | bytes 229408 | tf_op jit(solution)/shard_map/ppermute | solution.py:91
  340.4 4.9 %collective-permute-done.17 = bf16[4,56,512]{2,1,0:T(8,128)(2,1)S(1)} collective-permute-done((bf16[4,56,512]{2,1,0:T(8,128)(2,1)S(1)}, bf16[4,56,512]{2,1,0:T(8,128)(2,1)S(1)}, u32[]{:S(2)}, u32[]{:S(2)}) %collective-permute-start.17) | collective-permute-done | bytes 229408 | tf_op jit(solution)/shard_map/ppermute | solution.py:91
  372.7 11.1 %collective-permute-done.23 = bf16[4,152,512]{2,1,0:T(8,128)(2,1)} collective-permute-done((bf16[4,152,512]{2,1,0:T(8,128)(2,1)}, bf16[4,152,512]{2,1,0:T(8,128)(2,1)}, u32[]{:S(2)}, u32[]{:S(2)}) %collective-permute-start.23) | collective-permute-done | bytes 622624 | tf_op jit(solution)/shard_map/ppermute | solution.py:91
  392.3 6.4 %collective-permute-done.26 = bf16[1,152,512]{2,1,0:T(8,128)(2,1)S(1)} collective-permute-done((bf16[1,152,512]{2,1,0:T(8,128)(2,1)S(1)}, bf16[1,152,512]{2,1,0:T(8,128)(2,1)S(1)}, u32[]{:S(2)}, u32[]{:S(2)}) %collective-permute-start.26) | collective-permute-done | bytes 155680 | tf_op jit(solution)/shard_map/ppermute | solution.py:91
  (355 shorter events, 173.3 us)
Async XLA Ops:
  2.5 33.8 %collective-permute-start.7 = (bf16[144,512]{1,0:T(8,128)(2,1)S(1)}, bf16[144,512]{1,0:T(8,128)(2,1)}, u32[]{:S(2)}, u32[]{:S(2)}) collective-permute-start(bf16[144,512]{1,0:T(8,128)(2,1)S(1)} %pad_maximum_fusion.4), channel_id=1, source_target_pairs={{0,2},{1,3},{2,0},{3,1},{4,6},{5,7},{6,4},{7,5},{8,10},{9,11},{10,... | collective-permute-start | bytes 442376 | tf_op jit(solution)/shard_map/ppermute | solution.py:91
  5.5 32.1 %collective-permute-start.8 = (bf16[144,512]{1,0:T(8,128)(2,1)S(1)}, bf16[144,512]{1,0:T(8,128)(2,1)S(1)}, u32[]{:S(2)}, u32[]{:S(2)}) collective-permute-start(bf16[144,512]{1,0:T(8,128)(2,1)S(1)} %pad_maximum_fusion.4), channel_id=1, source_target_pairs={{0,4},{1,5},{2,6},{3,7},{4,0},{5,1},{6,2},{7,3},{8,12},{9,13},{10,... | collective-permute-start | bytes 442376 | tf_op jit(solution)/shard_map/ppermute | solution.py:91
  8.1 29.6 %collective-permute-start.9 = (bf16[144,512]{1,0:T(8,128)(2,1)S(1)}, bf16[144,512]{1,0:T(8,128)(2,1)S(1)}, u32[]{:S(2)}, u32[]{:S(2)}) collective-permute-start(bf16[144,512]{1,0:T(8,128)(2,1)S(1)} %pad_maximum_fusion.4), channel_id=1, source_target_pairs={{0,6},{1,7},{2,4},{3,5},{4,2},{5,3},{6,0},{7,1},{8,14},{9,15},{10,... | collective-permute-start | bytes 442376 | tf_op jit(solution)/shard_map/ppermute | solution.py:91
  16.3 10.6 %collective-permute-start = (bf16[56,512]{1,0:T(8,128)(2,1)S(1)}, bf16[56,512]{1,0:T(8,128)(2,1)S(1)}, u32[]{:S(2)}, u32[]{:S(2)}) collective-permute-start(bf16[56,512]{1,0:T(8,128)(2,1)S(1)} %fusion.61), channel_id=1, source_target_pairs={{0,2},{1,3},{2,0},{3,1},{4,6},{5,7},{6,4},{7,5},{8,10},{9,11},{10,... | collective-permute-start | bytes 172040 | tf_op jit(solution)/shard_map/ppermute | solution.py:91
  17.2 9.8 %collective-permute-start.1 = (bf16[56,512]{1,0:T(8,128)(2,1)S(1)}, bf16[56,512]{1,0:T(8,128)(2,1)S(1)}, u32[]{:S(2)}, u32[]{:S(2)}) collective-permute-start(bf16[56,512]{1,0:T(8,128)(2,1)S(1)} %fusion.61), channel_id=1, source_target_pairs={{0,4},{1,5},{2,6},{3,7},{4,0},{5,1},{6,2},{7,3},{8,12},{9,13},{10,... | collective-permute-start | bytes 172040 | tf_op jit(solution)/shard_map/ppermute | solution.py:91
  27.0 6.0 %collective-permute-start.2 = (bf16[56,512]{1,0:T(8,128)(2,1)S(1)}, bf16[56,512]{1,0:T(8,128)(2,1)S(1)}, u32[]{:S(2)}, u32[]{:S(2)}) collective-permute-start(bf16[56,512]{1,0:T(8,128)(2,1)S(1)} %fusion.61), channel_id=1, source_target_pairs={{0,6},{1,7},{2,4},{3,5},{4,2},{5,3},{6,0},{7,1},{8,14},{9,15},{10,... | collective-permute-start | bytes 172040 | tf_op jit(solution)/shard_map/ppermute | solution.py:91
  33.0 8.5 %collective-permute-start.3 = (bf16[4,56,512]{2,1,0:T(8,128)(2,1)S(1)}, bf16[4,56,512]{2,1,0:T(8,128)(2,1)S(1)}, u32[]{:S(2)}, u32[]{:S(2)}) collective-permute-start(bf16[4,56,512]{2,1,0:T(8,128)(2,1)S(1)} %bitcast_dynamic-update-slice_fusion.13), channel_id=1, source_target_pairs={{0,8},{1,9},{2,10},{3,11},{4,12},{5,13},{6,14},{7,15},{8,0},{9,1},... | collective-permute-start | bytes 688136 | tf_op jit(solution)/shard_map/ppermute | solution.py:91
  34.6 11.3 %collective-permute-start.4 = (bf16[4,56,512]{2,1,0:T(8,128)(2,1)S(1)}, bf16[4,56,512]{2,1,0:T(8,128)(2,1)S(1)}, u32[]{:S(2)}, u32[]{:S(2)}) collective-permute-start(bf16[4,56,512]{2,1,0:T(8,128)(2,1)S(1)} %bitcast_dynamic-update-slice_fusion.13), channel_id=1, source_target_pairs={{0,16},{1,17},{2,18},{3,19},{4,20},{5,21},{6,22},{7,23},{8,24},{9,... | collective-permute-start | bytes 688136 | tf_op jit(solution)/shard_map/ppermute | solution.py:91
  36.2 11.2 %collective-permute-start.5 = (bf16[4,56,512]{2,1,0:T(8,128)(2,1)S(1)}, bf16[4,56,512]{2,1,0:T(8,128)(2,1)S(1)}, u32[]{:S(2)}, u32[]{:S(2)}) collective-permute-start(bf16[4,56,512]{2,1,0:T(8,128)(2,1)S(1)} %bitcast_dynamic-update-slice_fusion.13), channel_id=1, source_target_pairs={{0,24},{1,25},{2,26},{3,27},{4,28},{5,29},{6,30},{7,31},{8,16},{9,... | collective-permute-start | bytes 688136 | tf_op jit(solution)/shard_map/ppermute | solution.py:91
  37.8 21.4 %collective-permute-start.10 = (bf16[4,144,512]{2,1,0:T(8,128)(2,1)S(1)}, bf16[4,144,512]{2,1,0:T(8,128)(2,1)S(1)}, u32[]{:S(2)}, u32[]{:S(2)}) collective-permute-start(bf16[4,144,512]{2,1,0:T(8,128)(2,1)S(1)} %bitcast_dynamic-update-slice_fusion.9), channel_id=1, source_target_pairs={{0,8},{1,9},{2,10},{3,11},{4,12},{5,13},{6,14},{7,15},{8,0},{9,1},... | collective-permute-start | bytes 1769480 | tf_op jit(solution)/shard_map/ppermute | solution.py:91
  39.3 30.2 %collective-permute-start.11 = (bf16[4,144,512]{2,1,0:T(8,128)(2,1)S(1)}, bf16[4,144,512]{2,1,0:T(8,128)(2,1)S(1)}, u32[]{:S(2)}, u32[]{:S(2)}) collective-permute-start(bf16[4,144,512]{2,1,0:T(8,128)(2,1)S(1)} %bitcast_dynamic-update-slice_fusion.9), channel_id=1, source_target_pairs={{0,16},{1,17},{2,18},{3,19},{4,20},{5,21},{6,22},{7,23},{8,24},{9,... | collective-permute-start | bytes 1769480 | tf_op jit(solution)/shard_map/ppermute | solution.py:91
  41.6 28.8 %collective-permute-start.12 = (bf16[4,144,512]{2,1,0:T(8,128)(2,1)S(1)}, bf16[4,144,512]{2,1,0:T(8,128)(2,1)S(1)}, u32[]{:S(2)}, u32[]{:S(2)}) collective-permute-start(bf16[4,144,512]{2,1,0:T(8,128)(2,1)S(1)} %bitcast_dynamic-update-slice_fusion.9), channel_id=1, source_target_pairs={{0,24},{1,25},{2,26},{3,27},{4,28},{5,29},{6,30},{7,31},{8,16},{9,... | collective-permute-start | bytes 1769480 | tf_op jit(solution)/shard_map/ppermute | solution.py:91
  47.5 23.8 %collective-permute-start.6 = (bf16[16,56,512]{2,1,0:T(8,128)(2,1)S(1)}, bf16[16,56,512]{2,1,0:T(8,128)(2,1)S(1)}, u32[]{:S(2)}, u32[]{:S(2)}) collective-permute-start(bf16[16,56,512]{2,1,0:T(8,128)(2,1)S(1)} %bitcast.306), channel_id=1, source_target_pairs={{0,1},{1,0},{2,3},{3,2},{4,5},{5,4},{6,7},{7,6},{8,9},{9,8},{10,11... | collective-permute-start | bytes 2752520 | tf_op jit(solution)/shard_map/ppermute | solution.py:91
  71.2 48.1 %collective-permute-start.13 = (bf16[16,144,512]{2,1,0:T(8,128)(2,1)}, bf16[16,144,512]{2,1,0:T(8,128)(2,1)}, u32[]{:S(2)}, u32[]{:S(2)}) collective-permute-start(bf16[16,144,512]{2,1,0:T(8,128)(2,1)} %bitcast.33), channel_id=1, source_target_pairs={{0,1},{1,0},{2,3},{3,2},{4,5},{5,4},{6,7},{7,6},{8,9},{9,8},{10,11... | collective-permute-start | bytes 7077896 | tf_op jit(solution)/shard_map/ppermute | solution.py:91
  117.8 58.5 %copy-start.56 = (f32[512]{0:T(512)}, f32[512]{0:T(512)S(1)}, u32[]{:S(2)}) copy-start(f32[512]{0:T(512)S(1)} %reshape.588) | copy-start | bytes 6148
  127.2 49.2 %copy-start.2 = (f32[1024,512]{0,1:T(8,128)}, f32[1024,512]{0,1:T(8,128)S(1)}, u32[]{:S(2)}) copy-start(f32[1024,512]{0,1:T(8,128)S(1)} %get-tuple-element.382) | copy-start | bytes 6291460
  127.2 49.1 %copy-start.36 = (f32[1024]{0:T(1024)}, f32[1024]{0:T(1024)S(1)}, u32[]{:S(2)}) copy-start(f32[1024]{0:T(1024)S(1)} %broadcast_multiply_fusion.8) | copy-start | bytes 12292
  127.5 48.8 %copy-start.50 = (f32[1024]{0:T(1024)}, f32[1024]{0:T(1024)S(1)}, u32[]{:S(2)}) copy-start(f32[1024]{0:T(1024)S(1)} %add_rsqrt_fusion.2) | copy-start | bytes 12292
  192.0 157.9 %collective-permute-start.21 = (bf16[16,152,512]{2,1,0:T(8,128)(2,1)}, bf16[16,152,512]{2,1,0:T(8,128)(2,1)}, u32[]{:S(2)}, u32[]{:S(2)}) collective-permute-start(bf16[16,152,512]{2,1,0:T(8,128)(2,1)} %fusion.37), channel_id=1, source_target_pairs={{0,1},{1,0},{2,3},{3,2},{4,5},{5,4},{6,7},{7,6},{8,9},{9,8},{10,11... | collective-permute-start | bytes 7471112 | tf_op jit(solution)/shard_map/ppermute | solution.py:91
  327.4 2.8 collective-permute-start.14
  331.8 8.5 %collective-permute-start.15 = (bf16[4,56,512]{2,1,0:T(8,128)(2,1)S(1)}, bf16[4,56,512]{2,1,0:T(8,128)(2,1)S(1)}, u32[]{:S(2)}, u32[]{:S(2)}) collective-permute-start(bf16[4,56,512]{2,1,0:T(8,128)(2,1)S(1)} %get-tuple-element.397), channel_id=1, source_target_pairs={{0,8},{1,9},{2,10},{3,11},{4,12},{5,13},{6,14},{7,15},{8,0},{9,1},... | collective-permute-start | bytes 688136 | tf_op jit(solution)/shard_map/ppermute | solution.py:91
  332.1 8.3 %collective-permute-start.16 = (bf16[4,56,512]{2,1,0:T(8,128)(2,1)S(1)}, bf16[4,56,512]{2,1,0:T(8,128)(2,1)S(1)}, u32[]{:S(2)}, u32[]{:S(2)}) collective-permute-start(bf16[4,56,512]{2,1,0:T(8,128)(2,1)S(1)} %get-tuple-element.399), channel_id=1, source_target_pairs={{0,16},{1,17},{2,18},{3,19},{4,20},{5,21},{6,22},{7,23},{8,24},{9,... | collective-permute-start | bytes 688136 | tf_op jit(solution)/shard_map/ppermute | solution.py:91
  333.8 11.5 %collective-permute-start.17 = (bf16[4,56,512]{2,1,0:T(8,128)(2,1)S(1)}, bf16[4,56,512]{2,1,0:T(8,128)(2,1)S(1)}, u32[]{:S(2)}, u32[]{:S(2)}) collective-permute-start(bf16[4,56,512]{2,1,0:T(8,128)(2,1)S(1)} %get-tuple-element.398), channel_id=1, source_target_pairs={{0,24},{1,25},{2,26},{3,27},{4,28},{5,29},{6,30},{7,31},{8,16},{9,... | collective-permute-start | bytes 688136 | tf_op jit(solution)/shard_map/ppermute | solution.py:91
  345.4 12.3 %collective-permute-start.18 = (bf16[1,56,512]{2,1,0:T(8,128)(2,1)S(1)}, bf16[1,56,512]{2,1,0:T(8,128)(2,1)S(1)}, u32[]{:S(2)}, u32[]{:S(2)}) collective-permute-start(bf16[1,56,512]{2,1,0:T(8,128)(2,1)S(1)} %get-tuple-element.408), channel_id=1, source_target_pairs={{0,2},{1,3},{2,0},{3,1},{4,6},{5,7},{6,4},{7,5},{8,10},{9,11},{10,... | collective-permute-start | bytes 172040 | tf_op jit(solution)/shard_map/ppermute | solution.py:91
  345.5 22.2 %collective-permute-start.19 = (bf16[1,56,512]{2,1,0:T(8,128)(2,1)S(1)}, bf16[1,56,512]{2,1,0:T(8,128)(2,1)S(1)}, u32[]{:S(2)}, u32[]{:S(2)}) collective-permute-start(bf16[1,56,512]{2,1,0:T(8,128)(2,1)S(1)} %get-tuple-element.410), channel_id=1, source_target_pairs={{0,4},{1,5},{2,6},{3,7},{4,0},{5,1},{6,2},{7,3},{8,12},{9,13},{10,... | collective-permute-start | bytes 172040 | tf_op jit(solution)/shard_map/ppermute | solution.py:91
  346.3 21.4 %collective-permute-start.20 = (bf16[1,56,512]{2,1,0:T(8,128)(2,1)S(1)}, bf16[1,56,512]{2,1,0:T(8,128)(2,1)S(1)}, u32[]{:S(2)}, u32[]{:S(2)}) collective-permute-start(bf16[1,56,512]{2,1,0:T(8,128)(2,1)S(1)} %get-tuple-element.409), channel_id=1, source_target_pairs={{0,6},{1,7},{2,4},{3,5},{4,2},{5,3},{6,0},{7,1},{8,14},{9,15},{10,... | collective-permute-start | bytes 172040 | tf_op jit(solution)/shard_map/ppermute | solution.py:91
  355.4 17.3 %collective-permute-start.22 = (bf16[4,152,512]{2,1,0:T(8,128)(2,1)}, bf16[4,152,512]{2,1,0:T(8,128)(2,1)}, u32[]{:S(2)}, u32[]{:S(2)}) collective-permute-start(bf16[4,152,512]{2,1,0:T(8,128)(2,1)} %get-tuple-element.387), channel_id=1, source_target_pairs={{0,8},{1,9},{2,10},{3,11},{4,12},{5,13},{6,14},{7,15},{8,0},{9,1},... | collective-permute-start | bytes 1867784 | tf_op jit(solution)/shard_map/ppermute | solution.py:91
  356.4 27.4 %collective-permute-start.23 = (bf16[4,152,512]{2,1,0:T(8,128)(2,1)}, bf16[4,152,512]{2,1,0:T(8,128)(2,1)}, u32[]{:S(2)}, u32[]{:S(2)}) collective-permute-start(bf16[4,152,512]{2,1,0:T(8,128)(2,1)} %get-tuple-element.389), channel_id=1, source_target_pairs={{0,16},{1,17},{2,18},{3,19},{4,20},{5,21},{6,22},{7,23},{8,24},{9,... | collective-permute-start | bytes 1867784 | tf_op jit(solution)/shard_map/ppermute | solution.py:91
  357.7 26.0 %collective-permute-start.24 = (bf16[4,152,512]{2,1,0:T(8,128)(2,1)}, bf16[4,152,512]{2,1,0:T(8,128)(2,1)}, u32[]{:S(2)}, u32[]{:S(2)}) collective-permute-start(bf16[4,152,512]{2,1,0:T(8,128)(2,1)} %get-tuple-element.388), channel_id=1, source_target_pairs={{0,24},{1,25},{2,26},{3,27},{4,28},{5,29},{6,30},{7,31},{8,16},{9,... | collective-permute-start | bytes 1867784 | tf_op jit(solution)/shard_map/ppermute | solution.py:91
  386.0 6.3 %collective-permute-start.25 = (bf16[1,152,512]{2,1,0:T(8,128)(2,1)S(1)}, bf16[1,152,512]{2,1,0:T(8,128)(2,1)S(1)}, u32[]{:S(2)}, u32[]{:S(2)}) collective-permute-start(bf16[1,152,512]{2,1,0:T(8,128)(2,1)S(1)} %get-tuple-element.405), channel_id=1, source_target_pairs={{0,2},{1,3},{2,0},{3,1},{4,6},{5,7},{6,4},{7,5},{8,10},{9,11},{10,... | collective-permute-start | bytes 466952 | tf_op jit(solution)/shard_map/ppermute | solution.py:91
  386.1 12.6 %collective-permute-start.26 = (bf16[1,152,512]{2,1,0:T(8,128)(2,1)S(1)}, bf16[1,152,512]{2,1,0:T(8,128)(2,1)S(1)}, u32[]{:S(2)}, u32[]{:S(2)}) collective-permute-start(bf16[1,152,512]{2,1,0:T(8,128)(2,1)S(1)} %get-tuple-element.407), channel_id=1, source_target_pairs={{0,4},{1,5},{2,6},{3,7},{4,0},{5,1},{6,2},{7,3},{8,12},{9,13},{10,... | collective-permute-start | bytes 466952 | tf_op jit(solution)/shard_map/ppermute | solution.py:91
  386.9 11.8 %collective-permute-start.27 = (bf16[1,152,512]{2,1,0:T(8,128)(2,1)S(1)}, bf16[1,152,512]{2,1,0:T(8,128)(2,1)S(1)}, u32[]{:S(2)}, u32[]{:S(2)}) collective-permute-start(bf16[1,152,512]{2,1,0:T(8,128)(2,1)S(1)} %get-tuple-element.406), channel_id=1, source_target_pairs={{0,6},{1,7},{2,4},{3,5},{4,2},{5,3},{6,0},{7,1},{8,14},{9,15},{10,... | collective-permute-start | bytes 466952 | tf_op jit(solution)/shard_map/ppermute | solution.py:91
  (67 other events, 391.0 us)
